TPU v7x, 256 devices: a whole 4x4x8 slice. The times are simulated.
256 devices in a mesh: req: 32 (over z, y), tp: 8 (over x, core).
Axes of the slice: x: 4, y: 4, z: 8, core: 2. Of those that a mesh axis runs over, the one named last changes fastest.
Arguments:
- hidden: bfloat16 [9472, 5120], P('req', 'tp'), may hold values from -6 to 6
- raw_q: bfloat16 [9472, 3072], P('req', 'tp'), may hold values from -70 to 70
- raw_k: bfloat16 [9472, 3072], P('req', 'tp'), may hold values from -70 to 70
- raw_v: bfloat16 [9472, 3072], P('req', 'tp'), may hold values from -6 to 6
- q_gain: float32 [3072], P('tp'), may hold values from 0.5 to 2
- k_gain: float32 [3072], P('tp'), may hold values from 0.5 to 2
- out_weight: bfloat16 [3072, 5120], P('tp'), may hold values from -0.109375 to 0.109375
- post_gain: float32 [5120], P('tp'), may hold values from 0.25 to 1.75
- prefix_keys: bfloat16 [32, 32, 128, 3072], P(None, 'req', None, 'tp'), may hold values from -420 to 420
- prefix_values: bfloat16 [32, 32, 128, 3072], P(None, 'req', None, 'tp'), may hold values from -6 to 6
- key_cache: bfloat16 [256, 128, 3072], P('req', None, 'tp'), may hold values from -420 to 420
- value_cache: bfloat16 [256, 128, 3072], P('req', None, 'tp'), may hold values from -6 to 6
- slot_owner: int32 [256], P('req'), may hold values from -1 to 255, as said below
- slot_page: int32 [256], P('req'), may hold values from 0 to 127, as said below
- cache_lengths: int32 [256], replicated, may hold values from 0 to 16384, as said below
- span_offsets: int32 [32], replicated, may hold values from 0 to 4096
Outputs:
- new_hidden: bfloat16 [9472, 5120], P('req', 'tp')
Inputs may be any that keep to these rules, and one draw needn't show every extreme that they name: Each pool slot holds one page of decode request slot_owner[s], or nothing where it is -1. No page of a request is held twice, and a request holding c pages holds pages 0 to c - 1. `slot_page`: 0 for a slot that holds nothing. `cache_lengths`: A request holding c pages of the pool has a length from (c - 1) * 128 + 1 to c * 128, and 0 where c = 0.
All inputs are finite; a program needn't handle non-finite values.
Results may differ from a plain program's by a relative error of at most 0.0076.
Values may be sent and summed in bfloat16 or wider, within the bound.
A program may use at most 128 MiB of HBM per device.

v0:
```python
import jax
import jax.numpy as jnp
from jax import lax
from jax.sharding import PartitionSpec as P

HD = 128
SPAN = 288
DEC = 8


EPSILON = 1e-06
THETA = 500000.0
NEGATIVE = -1e30


def rotate(values, positions):
    half_width = values.shape[-1] // 2
    frequency = THETA ** (-(jnp.arange(half_width, dtype=jnp.float32) * 2.0 / values.shape[-1]))
    angles = positions.astype(jnp.float32)[:, None] * frequency[None, :]
    cosine = jnp.cos(angles)[:, None, :]
    sine_part = jnp.sin(angles)[:, None, :]
    first_half = values[..., :half_width]
    second = values[..., half_width:]
    return jnp.concatenate(
        [first_half * cosine - second * sine_part, second * cosine + first_half * sine_part], -1
    )


def softmax_part(scores, key_mask, values, form):
    masked = jnp.where(key_mask, scores, NEGATIVE)
    top_score = jnp.max(masked, -1)
    exp_terms = jnp.where(key_mask, jnp.exp(masked - top_score[..., None]), 0.0)
    weight_sum = jnp.sum(exp_terms, -1)
    numerator = jnp.einsum(
        form, exp_terms.astype(jnp.bfloat16), values, preferred_element_type=jnp.float32
    )
    return (top_score, weight_sum, numerator)


def merge_parts(top_scores, weight_sums, numerators):
    best_score = jnp.max(top_scores, 0)
    factor = jnp.exp(top_scores - best_score[None])
    weight_sum = jnp.sum(factor * weight_sums, 0)
    numerator = jnp.sum(factor[..., None] * numerators, 0)
    return numerator / weight_sum[..., None]


def body(
    hidden,
    raw_q,
    raw_k,
    raw_v,
    q_gain,
    k_gain,
    out_weight,
    post_gain,
    prefix_keys,
    prefix_values,
    key_cache,
    value_cache,
    slot_owner,
    slot_page,
    cache_lengths,
    span_offsets,
):
    groups = lax.axis_size("req")
    my_group = lax.axis_index("req")
    tp_count = lax.axis_size("tp")
    rows_group = SPAN + DEC
    local_width = raw_q.shape[1]
    local_heads = local_width // HD
    requests = groups * DEC
    score_scale = HD ** (-0.5)
    page_rows = key_cache.shape[1]


    own_lengths = lax.dynamic_slice_in_dim(cache_lengths, my_group * DEC, DEC)
    positions = jnp.concatenate(
        [span_offsets[my_group] + jnp.arange(SPAN, dtype=jnp.int32), own_lengths]
    )
    float_query = raw_q.astype(jnp.float32)
    float_key = raw_k.astype(jnp.float32)
    query_power, key_power = lax.psum(
        (jnp.sum(float_query * float_query, 1), jnp.sum(float_key * float_key, 1)), "tp"
    )
    full_width = local_width * tp_count
    normed_query = (
        float_query * lax.rsqrt(query_power / full_width + EPSILON)[:, None] * q_gain[None, :]
    )
    normed_key = float_key * lax.rsqrt(key_power / full_width + EPSILON)[:, None] * k_gain[None, :]
    query = rotate(normed_query.reshape(rows_group, local_heads, HD), positions).astype(
        jnp.bfloat16
    )
    key_rows = rotate(normed_key.reshape(rows_group, local_heads, HD), positions).astype(
        jnp.bfloat16
    )
    value_rows = raw_v.reshape(rows_group, local_heads, HD)

    pages_here = prefix_keys.shape[1]
    block_rows = pages_here * page_rows
    outgoing = jnp.concatenate(
        [
            prefix_keys.reshape(groups, block_rows, local_width),
            jnp.broadcast_to(
                query[None, SPAN:].reshape(1, DEC, local_width), (groups, DEC, local_width)
            ),
        ],
        1,
    )
    incoming = lax.all_to_all(outgoing, "req", split_axis=0, concat_axis=0, tiled=True)
    own_values = lax.all_to_all(
        prefix_values.reshape(groups, block_rows, local_width),
        "req",
        split_axis=0,
        concat_axis=0,
        tiled=True,
    )
    prefix_len = groups * block_rows
    own_keys = incoming[:, :block_rows].reshape(prefix_len, local_width)
    own_values = own_values.reshape(prefix_len, local_width)
    decode_queries = incoming[:, block_rows:].reshape(requests, local_heads, HD)
    live_slot = slot_owner >= 0
    owner_index = jnp.maximum(slot_owner, 0)
    slot_queries = decode_queries[owner_index]
    slot_keys = key_cache.reshape(key_cache.shape[0], page_rows, local_heads, HD)
    slot_values = value_cache.reshape(value_cache.shape[0], page_rows, local_heads, HD)
    scores = (
        jnp.einsum("shd,sphd->shp", slot_queries, slot_keys, preferred_element_type=jnp.float32)
        * score_scale
    )
    key_pos = slot_page[:, None] * page_rows + jnp.arange(page_rows, dtype=jnp.int32)[None, :]
    key_mask = live_slot[:, None] & (key_pos < cache_lengths[owner_index][:, None])
    top_score, weight_sum, numerator = softmax_part(
        scores, key_mask[:, None, :], slot_values, "shp,sphd->shd"
    )
    member = slot_owner[None, :] == jnp.arange(requests, dtype=jnp.int32)[:, None]
    best_score = jnp.max(jnp.where(member[:, :, None], top_score[None], NEGATIVE), 1)
    factor = jnp.where(member[:, :, None], jnp.exp(top_score[None] - best_score[:, None]), 0.0)
    request_total = jnp.einsum("rsh,sh->rh", factor, weight_sum, precision=lax.Precision.HIGHEST)
    request_numerator = jnp.einsum(
        "rsh,shd->rhd", factor, numerator, precision=lax.Precision.HIGHEST
    )
    packed = jnp.concatenate(
        [request_numerator, best_score[..., None], request_total[..., None]], -1
    )
    back = lax.all_to_all(packed, "req", split_axis=0, concat_axis=0, tiled=True)
    back = back.reshape(groups, DEC, local_heads, HD + 2)
    own_scores = (
        jnp.sum(query[SPAN:].astype(jnp.float32) * key_rows[SPAN:].astype(jnp.float32), -1)
        * score_scale
    )
    decode_out = merge_parts(
        jnp.concatenate([back[..., HD], own_scores[None]], 0),
        jnp.concatenate([back[..., HD + 1], jnp.ones_like(own_scores)[None]], 0),
        jnp.concatenate([back[..., :HD], value_rows[SPAN:].astype(jnp.float32)[None]], 0),
    )

    span_query = query[:SPAN].reshape(SPAN, local_width)
    span_keys = key_rows[:SPAN].reshape(SPAN, local_width)
    causal = jnp.arange(SPAN)[:, None] >= jnp.arange(SPAN)[None, :]
    prefix_mask = jnp.arange(prefix_len, dtype=jnp.int32) < span_offsets[my_group]
    head_outs = []
    for head in range(local_heads):
        cols = slice(head * HD, (head + 1) * HD)
        head_query = span_query[:, cols]
        pre_scores = (
            jnp.einsum(
                "qd,kd->qk", head_query, own_keys[:, cols], preferred_element_type=jnp.float32
            )
            * score_scale
        )
        self_scores = (
            jnp.einsum(
                "qd,kd->qk", head_query, span_keys[:, cols], preferred_element_type=jnp.float32
            )
            * score_scale
        )
        pre_masked = jnp.where(prefix_mask[None, :], pre_scores, NEGATIVE)
        self_masked = jnp.where(causal, self_scores, NEGATIVE)
        top = jnp.maximum(jnp.max(pre_masked, -1), jnp.max(self_masked, -1))
        pre_exp = jnp.where(prefix_mask[None, :], jnp.exp(pre_masked - top[:, None]), 0.0)
        self_exp = jnp.where(causal, jnp.exp(self_masked - top[:, None]), 0.0)
        total = jnp.sum(pre_exp, -1) + jnp.sum(self_exp, -1)
        head_numerator = jnp.dot(
            pre_exp.astype(jnp.bfloat16), own_values[:, cols], preferred_element_type=jnp.float32
        ) + jnp.dot(
            self_exp.astype(jnp.bfloat16), raw_v[:SPAN, cols], preferred_element_type=jnp.float32
        )
        head_outs.append(head_numerator / total[:, None])
    span_out = jnp.concatenate(head_outs, 1)

    merged = jnp.concatenate([span_out, decode_out.reshape(DEC, local_width)], 0)
    attention = merged.astype(jnp.bfloat16)
    share_width = post_gain.shape[0]
    partial = jnp.dot(attention, out_weight, preferred_element_type=jnp.float32)
    my_share = lax.psum_scatter(
        partial.astype(jnp.bfloat16), "tp", scatter_dimension=1, tiled=True
    ).astype(jnp.float32)
    power = lax.psum(jnp.sum(my_share * my_share, 1), "tp")
    inverse = lax.rsqrt(power / (share_width * tp_count) + EPSILON)
    normed = my_share * inverse[:, None]
    return (hidden.astype(jnp.float32) + normed * post_gain[None, :]).astype(jnp.bfloat16)


def solution(mesh):
    return jax.shard_map(
        body,
        mesh=mesh,
        in_specs=(
            P("req", "tp"),
            P("req", "tp"),
            P("req", "tp"),
            P("req", "tp"),
            P("tp"),
            P("tp"),
            P("tp", None),
            P("tp"),
            P(None, "req", None, "tp"),
            P(None, "req", None, "tp"),
            P("req", None, "tp"),
            P("req", None, "tp"),
            P("req"),
            P("req"),
            P(),
            P(),
        ),
        out_specs=P("req", "tp"),
        check_vma=False,
    )
```

profile of v0, /device:TPU:1, one launch (start us, length us, event | category | flops | bytes accessed | tf_op | source)
XLA Modules:
  0.0 294.5 jit_solution(16382822483523100391)
XLA Ops:
  6.5 1.1 fusion.43
  7.6 1.1 fusion.45
  8.7 15.0 %all-reduce.1 = (f32[296]{0:T(512)S(1)}, f32[296]{0:T(512)S(1)}) all-reduce(f32[296]{0:T(512)S(1)} %fusion.43, f32[296]{0:T(512)S(1)} %fusion.45), channel_id=1, replica_groups=mesh['req'=32,'tp'=8] {'tp'}, use_global_device_ids=true, to_apply=%region_1.0 | all-reduce | flops 592 | bytes 4736 | tf_op jit(solution)/shard_map/psum | solution.py:83
  23.7 1.1 fusion.44
  25.0 1.2 dynamic_slice.7
  26.7 1.0 fusion.46
  28.0 0.9 dynamic_slice.8
  29.6 0.9 subtract_convert_fusion.1
  30.5 1.0 multiply_reduce_fusion
  31.9 84.1 %all_to_all.15 = bf16[32,136,384]{2,1,0:T(8,128)(2,1)S(1)} all-to-all(bf16[32,136,384]{2,1,0:T(8,128)(2,1)S(1)} %pad_maximum_fusion), channel_id=1, replica_groups=mesh['req'=32,'tp'=8] {'req'}, dimensions={0} | all-to-all | bytes 6684672 | tf_op jit(solution)/shard_map/all_to_all | solution.py:110
  116.1 6.0 %all-to-all-start.1 = ((bf16[32,128,384]{2,1,0:T(8,128)(2,1)}), bf16[32,128,384]{2,1,0:T(8,128)(2,1)}, u32[]{:S(2)}, u32[]{:S(2)}) async-start(bf16[32,128,384]{2,1,0:T(8,128)(2,1)} %bitcast.79), calls=%async_computation.1 | async-start | bytes 6291456 | tf_op jit(solution)/shard_map/all_to_all | solution.py:111
  122.1 2.3 copy.65
  125.1 2.3 copy.66
  127.4 1.5 fusion.55
  128.9 1.5 fusion.54
  132.4 0.7 bitcast_convert_fusion
  133.1 1.6 fusion.120
  134.7 1.6 fusion.122
  136.3 1.6 fusion.124
  137.8 0.8 reshape.267
  138.6 1.6 gather_fusion.1
  140.3 1.4 fusion.91
  141.7 0.8 fusion.103
  142.5 0.8 select_reduce_fusion
  143.2 0.8 fusion.104
  144.1 0.9 fusion.84
  145.0 1.6 fusion.89
  146.6 1.2 convolution_bitcast_fusion
  147.9 0.8 pad_maximum_fusion.1
  148.7 2.3 copy.67
  151.0 3.1 %reshape.298 = f32[32,1,3120]{2,1,0:T(1,128)} reshape(f32[256,3,130]{2,1,0:T(4,128)} %copy.67) | data formatting | bytes 798720
  155.0 3.0 %fusion.119 = (f32[288]{0:T(512)S(1)}, f32[288,4096]{1,0:T(8,128)}) fusion(bf16[4096,384]{1,0:T(8,128)(2,1)S(1)} %bitcast.73, bf16[288,384]{1,0:T(8,128)(2,1)S(1)} %bitcast.85, pred[4096]{0:T(1024)(128)(4,1)S(1)} %iota_compare_fusion.1), kind=kOutput, calls=%fused_computation.183 | convolution fusion | flops 305528544 | bytes 5846144 | tf_op jit(solution)/shard_map/qd,kd->qk/dot_general | solution.py:167
  158.1 3.1 %fusion.121 = (f32[288]{0:T(512)S(1)}, f32[288,4096]{1,0:T(8,128)}) fusion(bf16[4096,384]{1,0:T(8,128)(2,1)S(1)} %bitcast.74, bf16[288,384]{1,0:T(8,128)(2,1)S(1)} %bitcast.86, pred[4096]{0:T(1024)(128)(4,1)S(1)} %iota_compare_fusion.1), kind=kOutput, calls=%fused_computation.185 | convolution fusion | flops 305528544 | bytes 5846144 | tf_op jit(solution)/shard_map/qd,kd->qk/dot_general | solution.py:167
  161.2 3.0 %fusion.123 = (f32[288]{0:T(512)S(1)}, f32[288,4096]{1,0:T(8,128)}) fusion(bf16[4096,384]{1,0:T(8,128)(2,1)S(1)} %bitcast.75, bf16[288,384]{1,0:T(8,128)(2,1)S(1)} %bitcast.87, pred[4096]{0:T(1024)(128)(4,1)S(1)} %iota_compare_fusion.1), kind=kOutput, calls=%fused_computation.187 | convolution fusion | flops 305528544 | bytes 5846144 | tf_op jit(solution)/shard_map/qd,kd->qk/dot_general | solution.py:167
  164.2 23.4 %all-to-all-done.1 = bf16[32,128,384]{2,1,0:T(8,128)(2,1)} async-done(((bf16[32,128,384]{2,1,0:T(8,128)(2,1)}), bf16[32,128,384]{2,1,0:T(8,128)(2,1)}, u32[]{:S(2)}, u32[]{:S(2)}) %all-to-all-start.1) | async-done | bytes 3145760 | tf_op jit(solution)/shard_map/all_to_all | solution.py:111
  187.6 10.1 %all-to-all-start.2 = ((f32[32,1,3120]{2,1,0:T(1,128)}), f32[32,1,3120]{2,1,0:T(1,128)S(1)}, u32[]{:S(2)}, u32[]{:S(2)}) async-start(f32[32,1,3120]{2,1,0:T(1,128)} %reshape.298), calls=%async_computation.2 | async-start | bytes 819200 | tf_op jit(solution)/shard_map/all_to_all | solution.py:146
  197.8 3.6 %fusion.9 = f32[288,128]{1,0:T(8,128)S(1)} fusion(f32[288,4096]{1,0:T(8,128)} %get-tuple-element.30, f32[288]{0:T(512)S(1)} %max.26, pred[4096]{0:T(1024)(128)(4,1)S(1)} %iota_compare_fusion.1, bf16[4096,384]{1,0:T(8,128)(2,1)} %bitcast.4), kind=kOutput, calls=%fused_computation.19 | convolution fusion | flops 305528832 | bytes 5919872 | tf_op jit(solution)/shard_map/dot_general | solution.py:184
  201.5 4.3 %fusion.11 = f32[288,128]{1,0:T(8,128)S(1)} fusion(f32[288,4096]{1,0:T(8,128)} %get-tuple-element.38, f32[288]{0:T(512)S(1)} %max.25, pred[4096]{0:T(1024)(128)(4,1)S(1)} %iota_compare_fusion.1, bf16[4096,384]{1,0:T(8,128)(2,1)} %bitcast.4), kind=kOutput, calls=%fused_computation.20 | convolution fusion | flops 305528832 | bytes 5919872 | tf_op jit(solution)/shard_map/dot_general | solution.py:184
  206.6 2.6 fusion.3
  209.9 2.0 fusion.13
  212.8 1.6 reduce.3
  214.4 1.3 reshape.299
  217.5 3.9 %convolution_convert_fusion = bf16[296,5120]{1,0:T(8,128)(2,1)S(1)} fusion(bf16[384,5120]{1,0:T(8,128)(2,1)} %param.22, bf16[8,384]{1,0:T(8,128)(2,1)S(1)} %fusion.105, bf16[288,128]{1,0:T(8,128)(2,1)S(1)} %fusion.32, bf16[288,128]{1,0:T(8,128)(2,1)S(1)} %fusion.31, bf16[288,128]{1,0:T(8,128)(2,1)S(1)} %fusion.30), kind=kOutput, calls=%fused_computation.2 | convolution fusion | flops 1166344192 | bytes 7190528 | tf_op jit(solution)/shard_map/dot_general | solution.py:195
  221.4 3.6 %copy.84 = bf16[296,5120]{0,1:T(8,128)(2,1)} copy(bf16[296,5120]{1,0:T(8,128)(2,1)S(1)} %convolution_convert_fusion) | data formatting | bytes 6062080
  225.0 45.1 %reduce-scatter.4.cloned.1.call-done = bf16[640,296]{1,0:T(8,128)(2,1)} async-done(((bf16[5120,296]{1,0:T(8,128)(2,1)}), bf16[640,296]{1,0:T(8,128)(2,1)}) %reduce-scatter.4.cloned.1.call-update) | async-done | bytes 378896
  270.1 1.2 copy.85
  271.5 15.1 %psum.23 = f32[296]{0:T(512)S(1)} all-reduce(f32[296]{0:T(512)S(1)} %fusion.39), channel_id=1, replica_groups=mesh['req'=32,'tp'=8] {'tp'}, use_global_device_ids=true, to_apply=%region_25.26 | all-reduce | flops 296 | bytes 2368 | tf_op jit(solution)/shard_map/psum | solution.py:199
  286.7 1.0 fusion.42
  (113 shorter events, 9.9 us)
Async XLA Ops:
  28.0 3.6 %copy-start.1 = (bf16[32,1,128,384]{3,2,1,0:T(8,128)(2,1)S(1)}, bf16[32,1,128,384]{3,2,1,0:T(8,128)(2,1)}, u32[]{:S(2)}) copy-start(bf16[32,1,128,384]{3,2,1,0:T(8,128)(2,1)} %param.24) | copy-start | bytes 9437188
  30.5 1.0 copy-start.2
  30.5 1.0 copy-start.3
  30.5 1.0 copy-start.4
  30.5 1.0 copy-start.5
  116.1 8.3 %copy-start.18 = (s32[8]{0:T(128)S(1)}, s32[8]{0:T(128)}, u32[]{:S(2)}) copy-start(s32[8]{0:T(128)} %param.28) | copy-start | bytes 100
  116.1 8.4 %copy-start = (s32[256]{0:T(256)S(1)}, s32[256]{0:T(256)}, u32[]{:S(2)}) copy-start(s32[256]{0:T(256)} %param.30) | copy-start | bytes 3076
  116.1 71.6 %all-to-all-start.1 = ((bf16[32,128,384]{2,1,0:T(8,128)(2,1)}), bf16[32,128,384]{2,1,0:T(8,128)(2,1)}, u32[]{:S(2)}, u32[]{:S(2)}) async-start(bf16[32,128,384]{2,1,0:T(8,128)(2,1)} %bitcast.79), calls=%async_computation.1 | async-start | bytes 6291456 | tf_op jit(solution)/shard_map/all_to_all | solution.py:111
  122.1 9.0 %copy-start.20 = (s32[8]{0:T(128)S(1)}, s32[8]{0:T(128)}, u32[]{:S(2)}) copy-start(s32[8]{0:T(128)} %param.29) | copy-start | bytes 100
  124.4 11.8 %copy-start.13 = (s32[1024]{0:T(1024)}, s32[1024]{0:T(1024)S(1)}, u32[]{:S(2)}) copy-start(s32[1024]{0:T(1024)S(1)} %pad_clamp_fusion) | copy-start | bytes 12292
  128.9 7.4 %copy-start.6 = (bf16[36,8,3,128]{3,1,2,0:T(8,128)(2,1)}, bf16[36,8,3,128]{3,1,2,0:T(8,128)(2,1)S(1)}, u32[]{:S(2)}) copy-start(bf16[36,8,3,128]{3,1,2,0:T(8,128)(2,1)S(1)} %copy.115) | copy-start | bytes 663556
  154.1 0.9 copy-start.7
  155.0 3.0 %copy-start.17 = (f32[288]{0:T(512)S(1)}, f32[288]{0:T(512)}, u32[]{:S(2)}) copy-start(f32[288]{0:T(512)} %get-tuple-element.31) | copy-start | bytes 3460
  155.0 3.0 %copy-start.10 = (f32[288,288]{0,1:T(8,128)S(1)}, f32[288,288]{0,1:T(8,128)}, u32[]{:S(2)}) copy-start(f32[288,288]{0,1:T(8,128)} %get-tuple-element.32) | copy-start | bytes 995332
  187.6 13.8 %copy-start.16 = (f32[288]{0:T(512)S(1)}, f32[288]{0:T(512)}, u32[]{:S(2)}) copy-start(f32[288]{0:T(512)} %get-tuple-element.39) | copy-start | bytes 3460
  187.6 24.6 %all-to-all-start.2 = ((f32[32,1,3120]{2,1,0:T(1,128)}), f32[32,1,3120]{2,1,0:T(1,128)S(1)}, u32[]{:S(2)}, u32[]{:S(2)}) async-start(f32[32,1,3120]{2,1,0:T(1,128)} %reshape.298), calls=%async_computation.2 | async-start | bytes 819200 | tf_op jit(solution)/shard_map/all_to_all | solution.py:146
  197.7 72.4 %reduce-scatter.4.cloned.1.call-start = ((), (), s32[]{:S(2)}) async-start(), calls=%async_computation.4 | async-start | bytes 4423680
  197.8 8.1 %slice-start = ((s8[4718592]{0:T(1024)(128)(4,1)}), s8[4194304]{0:T(1024)(128)(4,1)S(1)}, s32[]{:S(2)}) async-start(s8[4718592]{0:T(1024)(128)(4,1)} %bitcast.66), calls=%async_computation.5 | async-start | bytes 8388608
  197.8 8.1 %slice-start.2 = ((s8[4718592]{0:T(1024)(128)(4,1)}), s8[4194304]{0:T(1024)(128)(4,1)S(1)}, s32[]{:S(2)}) async-start(s8[4718592]{0:T(1024)(128)(4,1)} %bitcast.68), calls=%async_computation.7 | async-start | bytes 8388608
  197.8 8.2 %slice-start.4 = ((s8[4718592]{0:T(1024)(128)(4,1)}), s8[4194304]{0:T(1024)(128)(4,1)S(1)}, s32[]{:S(2)}) async-start(s8[4718592]{0:T(1024)(128)(4,1)} %bitcast.70), calls=%async_computation.9 | async-start | bytes 8388608
  201.5 4.3 %copy-start.9 = (f32[288,288]{0,1:T(8,128)S(1)}, f32[288,288]{0,1:T(8,128)}, u32[]{:S(2)}) copy-start(f32[288,288]{0,1:T(8,128)} %get-tuple-element.40) | copy-start | bytes 995332
  201.5 4.4 %copy-start.15 = (f32[288]{0:T(512)S(1)}, f32[288]{0:T(512)}, u32[]{:S(2)}) copy-start(f32[288]{0:T(512)} %get-tuple-element.35) | copy-start | bytes 3460
  201.5 4.8 %slice-start.1 = ((s8[4718592]{0:T(1024)(128)(4,1)}), s8[524288]{0:T(1024)(128)(4,1)S(1)}, s32[]{:S(2)}) async-start(s8[4718592]{0:T(1024)(128)(4,1)} %bitcast.66), calls=%async_computation.6 | async-start | bytes 1048576
  201.5 4.9 %slice-start.3 = ((s8[4718592]{0:T(1024)(128)(4,1)}), s8[524288]{0:T(1024)(128)(4,1)S(1)}, s32[]{:S(2)}) async-start(s8[4718592]{0:T(1024)(128)(4,1)} %bitcast.68), calls=%async_computation.8 | async-start | bytes 1048576
  201.5 5.1 %slice-start.5 = ((s8[4718592]{0:T(1024)(128)(4,1)}), s8[524288]{0:T(1024)(128)(4,1)S(1)}, s32[]{:S(2)}) async-start(s8[4718592]{0:T(1024)(128)(4,1)} %bitcast.70), calls=%async_computation.10 | async-start | bytes 1048576
  206.6 2.7 copy-start.19
  206.6 3.2 %copy-start.8 = (f32[288,288]{0,1:T(8,128)S(1)}, f32[288,288]{0,1:T(8,128)}, u32[]{:S(2)}) copy-start(f32[288,288]{0,1:T(8,128)} %get-tuple-element.36) | copy-start | bytes 995332
  212.0 4.5 %copy-start.12 = (f32[8,3]{1,0:T(8,128)S(1)}, f32[8,3]{1,0:T(8,128)}, u32[]{:S(2)}) copy-start(f32[8,3]{1,0:T(8,128)} %get-tuple-element.12) | copy-start | bytes 292
  221.3 65.3 %copy-start.11 = (bf16[296,640]{1,0:T(8,128)(2,1)S(1)}, bf16[296,640]{1,0:T(8,128)(2,1)}, u32[]{:S(2)}) copy-start(bf16[296,640]{1,0:T(8,128)(2,1)} %param.16) | copy-start | bytes 1136644
  221.3 65.3 %copy-start.14 = (f32[640]{0:T(1024)S(1)}, f32[640]{0:T(1024)}, u32[]{:S(2)}) copy-start(f32[640]{0:T(1024)} %param.23) | copy-start | bytes 7684
Sparse Core Ops, SparseCore 0:
  225.1 44.9 reduce-scatter.3
where the time goes:
time: 296 us; the launch traced here: 294 us
  blocking collectives  114 us (39%)
  waiting for transfers between devices  68.5 us (23%)
  matrix products  33.6 us (11%)
  local copies, waits for them, and re-layouts  25.1 us (8%)
  other arithmetic  22.8 us (8%)
  starting transfers between devices  16.2 us (5%)
  between operations  14 us (5%)
    all_to_all x1, blocking collectives, body(): lax.all_to_all(outgoing, 'req', split_axis=0, concat_axis=0, tiled=True)  84.1 us
    unnamed x2, waiting for transfers between devices  45.1 us
    all_to_all x1, waiting for transfers between devices, body(): lax.all_to_all(prefix_values.reshape(groups, block_rows, local_width), 'r...  23.4 us
    psum x1, blocking collectives, body(): power = lax.psum(jnp.sum(my_share * my_share, 1), 'tp')  15.1 us
    unnamed x63, local copies, waits for them, and re-layouts  15.1 us
    psum x1, blocking collectives, body(): lax.psum((jnp.sum(float_query * float_query, 1), jnp.sum(float_key * floa...  15 us
    all_to_all x1, starting transfers between devices, body(): lax.all_to_all(packed, 'req', split_axis=0, concat_axis=0, tiled=True)  10.1 us
    dot_general x3, matrix products, body(): jnp.dot(pre_exp.astype(jnp.bfloat16), own_values[:, cols], preferred_elem...  9.94 us
  transfers between devices with their start and end apart: 3, of which 2 were waited for; matrix products, arithmetic and copies ran while one was open for 19% of the time, Pallas kernels for 0%

commit v1 on v0

--- a/solution.py
+++ b/solution.py
@@ -98,9 +98,11 @@
 
     pages_here = prefix_keys.shape[1]
     block_rows = pages_here * page_rows
+    half_rows = page_rows // 2
+    key_pages = prefix_keys.reshape(groups, block_rows, local_width)
     outgoing = jnp.concatenate(
         [
-            prefix_keys.reshape(groups, block_rows, local_width),
+            key_pages[:, :half_rows],
             jnp.broadcast_to(
                 query[None, SPAN:].reshape(1, DEC, local_width), (groups, DEC, local_width)
             ),
@@ -115,10 +117,16 @@
         concat_axis=0,
         tiled=True,
     )
-    prefix_len = groups * block_rows
-    own_keys = incoming[:, :block_rows].reshape(prefix_len, local_width)
-    own_values = own_values.reshape(prefix_len, local_width)
-    decode_queries = incoming[:, block_rows:].reshape(requests, local_heads, HD)
+    key_rest = lax.all_to_all(
+        key_pages[:, half_rows:], "req", split_axis=0, concat_axis=0, tiled=True
+    )
+    half_len = groups * half_rows
+    keys_front = incoming[:, :half_rows].reshape(half_len, local_width)
+    keys_back = key_rest.reshape(half_len, local_width)
+    values_grid = own_values.reshape(groups, block_rows, local_width)
+    values_front = values_grid[:, :half_rows].reshape(half_len, local_width)
+    values_back = values_grid[:, half_rows:].reshape(half_len, local_width)
+    decode_queries = incoming[:, half_rows:].reshape(requests, local_heads, HD)
     live_slot = slot_owner >= 0
     owner_index = jnp.maximum(slot_owner, 0)
     slot_queries = decode_queries[owner_index]
@@ -158,14 +166,32 @@
     span_query = query[:SPAN].reshape(SPAN, local_width)
     span_keys = key_rows[:SPAN].reshape(SPAN, local_width)
     causal = jnp.arange(SPAN)[:, None] >= jnp.arange(SPAN)[None, :]
-    prefix_mask = jnp.arange(prefix_len, dtype=jnp.int32) < span_offsets[my_group]
+    row_in_page = jnp.arange(half_rows, dtype=jnp.int32)[None, :]
+    page_start = jnp.arange(groups, dtype=jnp.int32)[:, None] * page_rows
+    front_mask = (page_start + row_in_page).reshape(-1) < span_offsets[my_group]
+    back_mask = (page_start + half_rows + row_in_page).reshape(-1) < span_offsets[my_group]
     head_outs = []
     for head in range(local_heads):
         cols = slice(head * HD, (head + 1) * HD)
         head_query = span_query[:, cols]
-        pre_scores = (
+        front_scores = (
             jnp.einsum(
-                "qd,kd->qk", head_query, own_keys[:, cols], preferred_element_type=jnp.float32
+                "qd,kd->qk", head_query, keys_front[:, cols], preferred_element_type=jnp.float32
+            )
+            * score_scale
+        )
+        front_masked = jnp.where(front_mask[None, :], front_scores, NEGATIVE)
+        front_top = jnp.max(front_masked, -1)
+        front_exp = jnp.where(
+            front_mask[None, :], jnp.exp(front_masked - front_top[:, None]), 0.0
+        )
+        front_total = jnp.sum(front_exp, -1)
+        front_numerator = jnp.dot(
+            front_exp.astype(jnp.bfloat16), values_front[:, cols], preferred_element_type=jnp.float32
+        )
+        back_scores = (
+            jnp.einsum(
+                "qd,kd->qk", head_query, keys_back[:, cols], preferred_element_type=jnp.float32
             )
             * score_scale
         )
@@ -175,16 +201,23 @@
             )
             * score_scale
         )
-        pre_masked = jnp.where(prefix_mask[None, :], pre_scores, NEGATIVE)
+        back_masked = jnp.where(back_mask[None, :], back_scores, NEGATIVE)
         self_masked = jnp.where(causal, self_scores, NEGATIVE)
-        top = jnp.maximum(jnp.max(pre_masked, -1), jnp.max(self_masked, -1))
-        pre_exp = jnp.where(prefix_mask[None, :], jnp.exp(pre_masked - top[:, None]), 0.0)
-        self_exp = jnp.where(causal, jnp.exp(self_masked - top[:, None]), 0.0)
-        total = jnp.sum(pre_exp, -1) + jnp.sum(self_exp, -1)
-        head_numerator = jnp.dot(
-            pre_exp.astype(jnp.bfloat16), own_values[:, cols], preferred_element_type=jnp.float32
+        back_top = jnp.maximum(jnp.max(back_masked, -1), jnp.max(self_masked, -1))
+        back_exp = jnp.where(back_mask[None, :], jnp.exp(back_masked - back_top[:, None]), 0.0)
+        self_exp = jnp.where(causal, jnp.exp(self_masked - back_top[:, None]), 0.0)
+        back_total = jnp.sum(back_exp, -1) + jnp.sum(self_exp, -1)
+        back_numerator = jnp.dot(
+            back_exp.astype(jnp.bfloat16), values_back[:, cols], preferred_element_type=jnp.float32
         ) + jnp.dot(
             self_exp.astype(jnp.bfloat16), raw_v[:SPAN, cols], preferred_element_type=jnp.float32
+        )
+        top = jnp.maximum(front_top, back_top)
+        front_factor = jnp.exp(front_top - top)
+        back_factor = jnp.exp(back_top - top)
+        total = front_factor * front_total + back_factor * back_total
+        head_numerator = (
+            front_factor[:, None] * front_numerator + back_factor[:, None] * back_numerator
         )
         head_outs.append(head_numerator / total[:, None])
     span_out = jnp.concatenate(head_outs, 1)
@@ -193,9 +226,7 @@
     attention = merged.astype(jnp.bfloat16)
     share_width = post_gain.shape[0]
     partial = jnp.dot(attention, out_weight, preferred_element_type=jnp.float32)
-    my_share = lax.psum_scatter(
-        partial.astype(jnp.bfloat16), "tp", scatter_dimension=1, tiled=True
-    ).astype(jnp.float32)
+    my_share = lax.psum_scatter(partial, "tp", scatter_dimension=1, tiled=True)
     power = lax.psum(jnp.sum(my_share * my_share, 1), "tp")
     inverse = lax.rsqrt(power / (share_width * tp_count) + EPSILON)
     normed = my_share * inverse[:, None]

time: 296 us -> 306 us (1.034)
  blocking collectives: 114 us -> 77.7 us
  waiting for transfers between devices: 68.5 us -> 104 us
  matrix products: 33.6 us -> 22.3 us
  local copies, waits for them, and re-layouts: 25.1 us -> 34.9 us
  other arithmetic: 22.8 us -> 30.4 us
  starting transfers between devices: 16.2 us -> 20.8 us
    reduce_scatter x0 -> x1, waiting for transfers between devices: none -> 48 us  [body(): my_share = lax.psum_scatter(partial, 'tp', scatter_dimension=1, tiled=True)]
    unnamed x2 -> x1, waiting for transfers between devices: 45.1 us -> 0.02 us
    all_to_all x1, blocking collectives: 84.1 us -> 49.7 us  [body(): lax.all_to_all(outgoing, 'req', split_axis=0, concat_axis=0, tiled=True)]
    all_to_all x0 -> x1, waiting for transfers between devices: none -> 19 us  [body(): lax.all_to_all(key_pages[:, half_rows:], 'req', split_axis=0, concat_axis...]
    dot_general x6 -> x12, matrix products: 19 us -> 8.13 us  [the longest x3 2.83 us: body(): jnp.einsum('qd,kd->qk', head_query, keys_back[:, cols], preferred_element...]
    all_to_all x1, waiting for transfers between devices: 0.01 us -> 6.78 us  [body(): lax.all_to_all(packed, 'req', split_axis=0, concat_axis=0, tiled=True)]
    all_to_all x0 -> x1, starting transfers between devices: none -> 6.72 us  [body(): lax.all_to_all(key_pages[:, half_rows:], 'req', split_axis=0, concat_axis...]
    all_to_all x1, waiting for transfers between devices: 23.4 us -> 29.7 us  [body(): lax.all_to_all(prefix_values.reshape(groups, block_rows, local_width), 'r...]
  transfers between devices with their start and end apart: 3 -> 4, of which waited for: 2 -> 4; matrix products, arithmetic and copies ran while one was open for 19% -> 19% of each run, Pallas kernels for 0% -> 0%
where the time goes in v1:
time: 306 us; the launch traced here: 304 us
  waiting for transfers between devices  104 us (34%)
  blocking collectives  77.7 us (25%)
  local copies, waits for them, and re-layouts  34.9 us (11%)
  other arithmetic  30.4 us (10%)
  matrix products  22.3 us (7%)
  starting transfers between devices  20.8 us (7%)
  between operations  14.3 us (5%)
    all_to_all x1, blocking collectives, body(): lax.all_to_all(outgoing, 'req', split_axis=0, concat_axis=0, tiled=True)  49.7 us
    reduce_scatter x1, waiting for transfers between devices, body(): my_share = lax.psum_scatter(partial, 'tp', scatter_dimension=1, tiled=True)  48 us
    all_to_all x1, waiting for transfers between devices, body(): lax.all_to_all(prefix_values.reshape(groups, block_rows, local_width), 'r...  29.7 us
    all_to_all x1, waiting for transfers between devices, body(): lax.all_to_all(key_pages[:, half_rows:], 'req', split_axis=0, concat_axis...  19 us
    unnamed x141, local copies, waits for them, and re-layouts  17.6 us
    psum x1, blocking collectives, body(): lax.psum((jnp.sum(float_query * float_query, 1), jnp.sum(float_key * floa...  15 us
    psum x1, blocking collectives, body(): power = lax.psum(jnp.sum(my_share * my_share, 1), 'tp')  13.1 us
    all_to_all x1, starting transfers between devices, body(): lax.all_to_all(packed, 'req', split_axis=0, concat_axis=0, tiled=True)  7.82 us
  transfers between devices with their start and end apart: 4, of which 4 were waited for; matrix products, arithmetic and copies ran while one was open for 19% of the time, Pallas kernels for 0%

profile of v1, /device:TPU:1, one launch (start us, length us, event | category | flops | bytes accessed | tf_op | source)
XLA Modules:
  0.0 303.9 jit_solution(11600340176925719552)
XLA Ops:
  6.6 1.4 dynamic_slice.8
  8.6 1.1 fusion.117
  9.7 1.1 fusion.119
  10.8 15.0 %all-reduce.1 = (f32[296]{0:T(512)S(1)}, f32[296]{0:T(512)S(1)}) all-reduce(f32[296]{0:T(512)S(1)} %fusion.117, f32[296]{0:T(512)S(1)} %fusion.119), channel_id=1, replica_groups=mesh['req'=32,'tp'=8] {'tp'}, use_global_device_ids=true, to_apply=%region_1.0 | all-reduce | flops 592 | bytes 4736 | tf_op jit(solution)/shard_map/psum | solution.py:83
  25.8 1.1 fusion.120
  30.7 1.5 fusion.215
  32.5 49.7 %all_to_all.20 = bf16[32,72,384]{2,1,0:T(8,128)(2,1)S(1)} all-to-all(bf16[32,72,384]{2,1,0:T(8,128)(2,1)S(1)} %pad_maximum_fusion), channel_id=1, replica_groups=mesh['req'=32,'tp'=8] {'req'}, dimensions={0} | all-to-all | bytes 3538944 | tf_op jit(solution)/shard_map/all_to_all | solution.py:112
  82.2 6.7 %all-to-all-start.1 = ((bf16[32,64,384]{2,1,0:T(8,128)(2,1)}), bf16[32,64,384]{2,1,0:T(8,128)(2,1)S(1)}, u32[]{:S(2)}, u32[]{:S(2)}) async-start(bf16[32,64,384]{2,1,0:T(8,128)(2,1)} %get-tuple-element.28), calls=%async_computation.1 | async-start | bytes 3145728 | tf_op jit(solution)/shard_map/all_to_all | solution.py:120
  89.6 2.3 copy.65
  91.9 2.3 copy.66
  96.3 1.4 fusion.172
  98.4 1.6 fusion.170
  101.4 1.5 copy.67
  102.9 2.1 reshape.427
  105.0 19.0 %all-to-all-done.1 = bf16[32,64,384]{2,1,0:T(8,128)(2,1)S(1)} async-done(((bf16[32,64,384]{2,1,0:T(8,128)(2,1)}), bf16[32,64,384]{2,1,0:T(8,128)(2,1)S(1)}, u32[]{:S(2)}, u32[]{:S(2)}) %all-to-all-start.1) | async-done | bytes 1572896 | tf_op jit(solution)/shard_map/all_to_all | solution.py:120
  124.0 7.8 %all-to-all-start.3 = ((f32[32,1,3120]{2,1,0:T(1,128)}), f32[32,1,3120]{2,1,0:T(1,128)S(1)}, u32[]{:S(2)}, u32[]{:S(2)}) async-start(f32[32,1,3120]{2,1,0:T(1,128)} %reshape.427), calls=%async_computation.3 | async-start | bytes 819200 | tf_op jit(solution)/shard_map/all_to_all | solution.py:154
  132.8 1.4 fusion.128
  134.7 1.0 fusion.220
  135.7 1.0 fusion.222
  136.8 6.8 %all-to-all-done.3 = f32[32,1,3120]{2,1,0:T(1,128)S(1)} async-done(((f32[32,1,3120]{2,1,0:T(1,128)}), f32[32,1,3120]{2,1,0:T(1,128)S(1)}, u32[]{:S(2)}, u32[]{:S(2)}) %all-to-all-start.3) | async-done | bytes 399392 | tf_op jit(solution)/shard_map/all_to_all | solution.py:154
  144.3 6.0 %all-to-all-start.2 = ((bf16[32,128,384]{2,1,0:T(8,128)(2,1)}), bf16[32,128,384]{2,1,0:T(8,128)(2,1)S(1)}, u32[]{:S(2)}, u32[]{:S(2)}) async-start(bf16[32,128,384]{2,1,0:T(8,128)(2,1)} %bitcast.75), calls=%async_computation.2 | async-start | bytes 6291456 | tf_op jit(solution)/shard_map/all_to_all | solution.py:113
  150.5 1.4 bitcast_convert_fusion
  151.9 1.1 fusion.218
  153.1 1.6 fusion.217
  158.3 0.9 fusion.140
  160.2 1.3 fusion.8
  163.9 2.1 fusion.6
  168.4 2.4 reduce.3
  170.8 3.3 %reshape.428 = f32[256,3,130]{2,1,0:T(4,128)} reshape(f32[32,3120]{1,0:T(8,128)} %reduce.3) | data formatting | bytes 798720
  174.1 1.4 copy.111
  175.6 1.6 fusion.216
  177.1 1.2 copy.69
  178.3 1.3 copy.72
  179.6 1.3 multiply_bitcast_fusion
  180.9 1.3 copy.73
  182.2 1.4 copy.71
  183.6 1.8 copy.75
  185.4 1.4 multiply_reduce_fusion.2
  186.8 1.4 copy.74
  188.3 1.0 fusion.121
  189.4 29.7 %all-to-all-done.2 = bf16[32,128,384]{2,1,0:T(8,128)(2,1)S(1)} async-done(((bf16[32,128,384]{2,1,0:T(8,128)(2,1)}), bf16[32,128,384]{2,1,0:T(8,128)(2,1)S(1)}, u32[]{:S(2)}, u32[]{:S(2)}) %all-to-all-start.2) | async-done | bytes 3145760 | tf_op jit(solution)/shard_map/all_to_all | solution.py:113
  219.6 1.2 copy-done.8
  227.2 1.1 copy-done.17
  228.2 4.4 %fusion.130 = f32[296,5120]{1,0:T(8,128)} fusion(bf16[384,5120]{1,0:T(8,128)(2,1)S(1)} %copy-done.17, bf16[8,384]{1,0:T(8,128)(2,1)S(1)} %fusion.186, bf16[288,128]{1,0:T(8,128)(2,1)S(1)} %fusion.102, bf16[288,128]{1,0:T(8,128)(2,1)S(1)} %fusion.99, bf16[288,128]{1,0:T(8,128)(2,1)S(1)} %fusion.96), kind=kOutput, calls=%fused_computation.128 | convolution fusion | flops 1164828672 | bytes 10221568 | tf_op jit(solution)/shard_map/dot_general | solution.py:228
  232.6 48.0 %reduce-scatter.2.cloned.1.call-done = f32[296,640]{1,0:T(8,128)} async-done(((f32[296,5120]{1,0:T(8,128)}), f32[296,640]{1,0:T(8,128)}) %reduce-scatter.2.cloned.1.call-update) | async-done | bytes 757776 | tf_op jit(solution)/shard_map/reduce_scatter | solution.py:229
  280.6 1.3 multiply_reduce_fusion
  281.9 13.1 %psum.23 = f32[296]{0:T(512)S(1)} all-reduce(f32[296]{0:T(512)S(1)} %multiply_reduce_fusion), channel_id=1, replica_groups=mesh['req'=32,'tp'=8] {'tp'}, use_global_device_ids=true, to_apply=%region_31.32 | all-reduce | flops 296 | bytes 2368 | tf_op jit(solution)/shard_map/psum | solution.py:230
  295.0 2.1 add_convert_fusion
  (204 shorter events, 27.7 us)
Async XLA Ops:
  6.5 20.5 %copy-start.28 = (bf16[296,384]{1,0:T(8,128)(2,1)S(1)}, bf16[296,384]{1,0:T(8,128)(2,1)}, u32[]{:S(2)}) copy-start(bf16[296,384]{1,0:T(8,128)(2,1)} %param.17) | copy-start | bytes 681988
  6.5 21.5 %copy-start = (s32[256]{0:T(256)S(1)}, s32[256]{0:T(256)}, u32[]{:S(2)}) copy-start(s32[256]{0:T(256)} %param.30) | copy-start | bytes 3076
  28.8 1.9 copy-start.18
  82.2 13.5 %copy-start.13 = (bf16[32,72,384]{2,1,0:T(8,128)(2,1)}, bf16[32,72,384]{2,1,0:T(8,128)(2,1)S(1)}, u32[]{:S(2)}) copy-start(bf16[32,72,384]{2,1,0:T(8,128)(2,1)S(1)} %all_to_all.20) | copy-start | bytes 5308420
  82.2 6.7 %copy-start.60 = (s32[8]{0:T(128)S(1)}, s32[8]{0:T(128)}, u32[]{:S(2)}) copy-start(s32[8]{0:T(128)} %param.28) | copy-start | bytes 100
  82.2 41.9 %all-to-all-start.1 = ((bf16[32,64,384]{2,1,0:T(8,128)(2,1)}), bf16[32,64,384]{2,1,0:T(8,128)(2,1)S(1)}, u32[]{:S(2)}, u32[]{:S(2)}) async-start(bf16[32,64,384]{2,1,0:T(8,128)(2,1)} %get-tuple-element.28), calls=%async_computation.1 | async-start | bytes 3145728 | tf_op jit(solution)/shard_map/all_to_all | solution.py:120
  88.9 5.8 %copy-start.63 = (s32[8]{0:T(128)S(1)}, s32[8]{0:T(128)}, u32[]{:S(2)}) copy-start(s32[8]{0:T(128)} %param.29) | copy-start | bytes 100
  100.6 31.3 %copy-start.61 = (s32[32]{0:T(128)S(1)}, s32[32]{0:T(128)}, u32[]{:S(2)}) copy-start(s32[32]{0:T(128)} %broadcast_add_fusion) | copy-start | bytes 388
  100.6 32.2 %copy-start.24 = (bf16[296,3,64]{2,1,0:T(4,128)(2,1)S(1)}, bf16[296,3,64]{2,1,0:T(4,128)(2,1)}, u32[]{:S(2)}) copy-start(bf16[296,3,64]{2,1,0:T(4,128)(2,1)} %copy-done.23) | copy-start | bytes 340996
  101.4 32.8 %copy-start.20 = (bf16[296,3,64]{2,1,0:T(4,128)(2,1)S(1)}, bf16[296,3,64]{2,1,0:T(4,128)(2,1)}, u32[]{:S(2)}) copy-start(bf16[296,3,64]{2,1,0:T(4,128)(2,1)} %copy-done.19) | copy-start | bytes 340996
  101.4 32.8 %copy-start.22 = (bf16[296,3,64]{2,1,0:T(4,128)(2,1)S(1)}, bf16[296,3,64]{2,1,0:T(4,128)(2,1)}, u32[]{:S(2)}) copy-start(bf16[296,3,64]{2,1,0:T(4,128)(2,1)} %copy-done.21) | copy-start | bytes 340996
  124.0 12.7 %copy-start.15 = (bf16[32,64,384]{2,1,0:T(8,128)(2,1)}, bf16[32,64,384]{2,1,0:T(8,128)(2,1)S(1)}, u32[]{:S(2)}) copy-start(bf16[32,64,384]{2,1,0:T(8,128)(2,1)S(1)} %all-to-all-done.1) | copy-start | bytes 4718596
  124.0 19.5 %all-to-all-start.3 = ((f32[32,1,3120]{2,1,0:T(1,128)}), f32[32,1,3120]{2,1,0:T(1,128)S(1)}, u32[]{:S(2)}, u32[]{:S(2)}) async-start(f32[32,1,3120]{2,1,0:T(1,128)} %reshape.427), calls=%async_computation.3 | async-start | bytes 819200 | tf_op jit(solution)/shard_map/all_to_all | solution.py:154
  132.7 30.4 %copy-start.33 = (pred[2048]{0:T(1024)(128)(4,1)}, pred[2048]{0:T(1024)(128)(4,1)S(1)}, u32[]{:S(2)}) copy-start(pred[2048]{0:T(1024)(128)(4,1)S(1)} %lt.49) | copy-start | bytes 6148
  132.8 27.3 %copy-start.35 = (pred[2048]{0:T(1024)(128)(4,1)}, pred[2048]{0:T(1024)(128)(4,1)S(1)}, u32[]{:S(2)}) copy-start(pred[2048]{0:T(1024)(128)(4,1)S(1)} %lt.52) | copy-start | bytes 6148
  134.3 9.3 %copy-start.32 = (bf16[36,8,3,128]{3,1,2,0:T(8,128)(2,1)}, bf16[36,8,3,128]{3,1,2,0:T(8,128)(2,1)S(1)}, u32[]{:S(2)}) copy-start(bf16[36,8,3,128]{3,1,2,0:T(8,128)(2,1)S(1)} %copy.112) | copy-start | bytes 663556
  144.3 74.9 %all-to-all-start.2 = ((bf16[32,128,384]{2,1,0:T(8,128)(2,1)}), bf16[32,128,384]{2,1,0:T(8,128)(2,1)S(1)}, u32[]{:S(2)}, u32[]{:S(2)}) async-start(bf16[32,128,384]{2,1,0:T(8,128)(2,1)} %bitcast.75), calls=%async_computation.2 | async-start | bytes 6291456 | tf_op jit(solution)/shard_map/all_to_all | solution.py:113
  150.3 130.4 %reduce-scatter.2.cloned.1.call-start = ((), (), s32[]{:S(2)}) async-start(), calls=%async_computation.5 | async-start | bytes 6819840 | tf_op jit(solution)/shard_map/reduce_scatter | solution.py:229
  150.5 4.2 %copy-start.16 = (bf16[32,64,384]{2,1,0:T(8,128)(2,1)S(1)}, bf16[32,64,384]{2,1,0:T(8,128)(2,1)}, u32[]{:S(2)}) copy-start(bf16[32,64,384]{2,1,0:T(8,128)(2,1)} %copy-done.15) | copy-start | bytes 4718596
  154.7 5.5 %copy-start.1 = (f32[288,2048]{1,0:T(8,128)}, f32[288,2048]{1,0:T(8,128)S(1)}, u32[]{:S(2)}) copy-start(f32[288,2048]{1,0:T(8,128)S(1)} %get-tuple-element.46) | copy-start | bytes 7077892
  154.7 12.5 %copy-start.37 = (f32[288]{0:T(512)}, f32[288]{0:T(512)S(1)}, u32[]{:S(2)}) copy-start(f32[288]{0:T(512)S(1)} %max.94) | copy-start | bytes 3460
  155.3 4.8 %copy-start.3 = (f32[288,2048]{1,0:T(8,128)}, f32[288,2048]{1,0:T(8,128)S(1)}, u32[]{:S(2)}) copy-start(f32[288,2048]{1,0:T(8,128)S(1)} %get-tuple-element.54) | copy-start | bytes 7077892
  155.4 2.0 copy-start.62
  155.4 11.2 %copy-start.39 = (f32[288]{0:T(512)}, f32[288]{0:T(512)S(1)}, u32[]{:S(2)}) copy-start(f32[288]{0:T(512)S(1)} %max.92) | copy-start | bytes 3460
  156.0 5.5 %copy-start.7 = (f32[288,2048]{1,0:T(8,128)}, f32[288,2048]{1,0:T(8,128)S(1)}, u32[]{:S(2)}) copy-start(f32[288,2048]{1,0:T(8,128)S(1)} %get-tuple-element.50) | copy-start | bytes 7077892
  156.0 10.0 %copy-start.41 = (f32[288]{0:T(512)}, f32[288]{0:T(512)S(1)}, u32[]{:S(2)}) copy-start(f32[288]{0:T(512)S(1)} %max.90) | copy-start | bytes 3460
  162.5 4.7 %copy-start.43 = (f32[288]{0:T(512)}, f32[288]{0:T(512)S(1)}, u32[]{:S(2)}) copy-start(f32[288]{0:T(512)S(1)} %get-tuple-element.61) | copy-start | bytes 3460
  163.1 2.9 copy-start.9
  163.1 3.5 %copy-start.45 = (f32[288]{0:T(512)}, f32[288]{0:T(512)S(1)}, u32[]{:S(2)}) copy-start(f32[288]{0:T(512)S(1)} %get-tuple-element.59) | copy-start | bytes 3460
  163.7 2.3 copy-start.11
  163.8 2.3 copy-start.47
  163.9 4.5 %copy-start.27 = (f32[32,1,3120]{2,1,0:T(1,128)S(1)}, f32[32,1,3120]{2,1,0:T(1,128)}, u32[]{:S(2)}) copy-start(f32[32,1,3120]{2,1,0:T(1,128)} %copy-done.26) | copy-start | bytes 1198084
  174.1 5.5 %copy-start.49 = (f32[8,3]{1,0:T(8,128)S(1)}, f32[8,3]{1,0:T(8,128)}, u32[]{:S(2)}) copy-start(f32[8,3]{1,0:T(8,128)} %get-tuple-element.24) | copy-start | bytes 292
  189.4 30.2 %copy-start.36 = (pred[2048]{0:T(1024)(128)(4,1)S(1)}, pred[2048]{0:T(1024)(128)(4,1)}, u32[]{:S(2)}) copy-start(pred[2048]{0:T(1024)(128)(4,1)} %copy-done.35) | copy-start | bytes 6148
  189.4 30.2 %copy-start.42 = (f32[288]{0:T(512)S(1)}, f32[288]{0:T(512)}, u32[]{:S(2)}) copy-start(f32[288]{0:T(512)} %copy-done.41) | copy-start | bytes 3460
  189.4 30.2 %copy-start.57 = (f32[288]{0:T(512)S(1)}, f32[288]{0:T(512)}, u32[]{:S(2)}) copy-start(f32[288]{0:T(512)} %get-tuple-element.15) | copy-start | bytes 3460
  189.4 30.2 %copy-start.66 = (f32[288,128]{1,0:T(8,128)S(1)}, f32[288,128]{1,0:T(8,128)}, u32[]{:S(2)}) copy-start(f32[288,128]{1,0:T(8,128)} %fusion.142) | copy-start | bytes 442372
  219.5 2.1 copy-start.4
  219.5 2.1 copy-start.40
  219.5 2.1 copy-start.58
  219.5 2.1 copy-start.65
  222.2 1.9 copy-start.12
  222.2 1.8 copy-start.34
  222.2 1.8 copy-start.48
  222.2 1.8 copy-start.51
  226.0 2.3 copy-start.17
  232.6 62.4 %copy-start.31 = (bf16[296,640]{1,0:T(8,128)(2,1)S(1)}, bf16[296,640]{1,0:T(8,128)(2,1)}, u32[]{:S(2)}) copy-start(bf16[296,640]{1,0:T(8,128)(2,1)} %param.16) | copy-start | bytes 1136644
  232.6 62.4 %copy-start.50 = (f32[640]{0:T(1024)S(1)}, f32[640]{0:T(1024)}, u32[]{:S(2)}) copy-start(f32[640]{0:T(1024)} %param.23) | copy-start | bytes 7684
  (23 other events, 34.9 us)
Sparse Core Ops, SparseCore 0:
  232.7 47.8 reduce-scatter.1

commit v2 on v0

--- a/solution.py
+++ b/solution.py
@@ -192,10 +192,14 @@
     merged = jnp.concatenate([span_out, decode_out.reshape(DEC, local_width)], 0)
     attention = merged.astype(jnp.bfloat16)
     share_width = post_gain.shape[0]
-    partial = jnp.dot(attention, out_weight, preferred_element_type=jnp.float32)
-    my_share = lax.psum_scatter(
-        partial.astype(jnp.bfloat16), "tp", scatter_dimension=1, tiled=True
-    ).astype(jnp.float32)
+    column_blocks = out_weight.reshape(local_width, tp_count, share_width)
+    partial = jnp.einsum(
+        "rk,kcn->crn", attention, column_blocks, preferred_element_type=jnp.float32
+    )
+    pieces = lax.all_to_all(
+        partial.astype(jnp.bfloat16), "tp", split_axis=0, concat_axis=0, tiled=True
+    )
+    my_share = jnp.sum(pieces.astype(jnp.float32), 0)
     power = lax.psum(jnp.sum(my_share * my_share, 1), "tp")
     inverse = lax.rsqrt(power / (share_width * tp_count) + EPSILON)
     normed = my_share * inverse[:, None]

time: 296 us -> 279 us (0.943)
  blocking collectives: 114 us -> 161 us
  waiting for transfers between devices: 68.5 us -> 23.4 us
  between operations: 14 us -> 0.61 us
  local copies, waits for them, and re-layouts: 25.1 us -> 20.2 us
    all_to_all x0 -> x1, blocking collectives: none -> 48.9 us  [body(): lax.all_to_all(partial.astype(jnp.bfloat16), 'tp', split_axis=0, concat_a...]
    unnamed x2 -> x0, waiting for transfers between devices: 45.1 us -> none
    unnamed x63 -> x61, local copies, waits for them, and re-layouts: 15.1 us -> 10.2 us
  transfers between devices with their start and end apart: 3 -> 2, of which waited for: 2 -> 1; matrix products, arithmetic and copies ran while one was open for 19% -> 20% of each run, Pallas kernels for 0% -> 0%
where the time goes in v2:
time: 279 us; the launch traced here: 278 us
  blocking collectives  161 us (58%)
  matrix products  33.6 us (12%)
  waiting for transfers between devices  23.4 us (8%)
  other arithmetic  23.2 us (8%)
  local copies, waits for them, and re-layouts  20.2 us (7%)
  starting transfers between devices  16 us (6%)
    all_to_all x1, blocking collectives, body(): lax.all_to_all(outgoing, 'req', split_axis=0, concat_axis=0, tiled=True)  84.1 us
    all_to_all x1, blocking collectives, body(): lax.all_to_all(partial.astype(jnp.bfloat16), 'tp', split_axis=0, concat_a...  48.9 us
    all_to_all x1, waiting for transfers between devices, body(): lax.all_to_all(prefix_values.reshape(groups, block_rows, local_width), 'r...  23.4 us
    psum x1, blocking collectives, body(): lax.psum((jnp.sum(float_query * float_query, 1), jnp.sum(float_key * floa...  15 us
    psum x1, blocking collectives, body(): power = lax.psum(jnp.sum(my_share * my_share, 1), 'tp')  12.7 us
    unnamed x61, local copies, waits for them, and re-layouts  10.2 us
    dot_general x3, matrix products, body(): jnp.dot(pre_exp.astype(jnp.bfloat16), own_values[:, cols], preferred_elem...  9.94 us
    all_to_all x1, starting transfers between devices, body(): lax.all_to_all(packed, 'req', split_axis=0, concat_axis=0, tiled=True)  9.92 us
  transfers between devices with their start and end apart: 2, of which 1 were waited for; matrix products, arithmetic and copies ran while one was open for 20% of the time, Pallas kernels for 0%

profile of v2, /device:TPU:1, one launch (start us, length us, event | category | flops | bytes accessed | tf_op | source)
XLA Modules:
  0.0 277.7 jit_solution(1363530600278134658)
XLA Ops:
  0.0 1.1 fusion.44
  1.1 1.1 fusion.46
  2.2 15.0 %all-reduce.1 = (f32[296]{0:T(512)S(1)}, f32[296]{0:T(512)S(1)}) all-reduce(f32[296]{0:T(512)S(1)} %fusion.44, f32[296]{0:T(512)S(1)} %fusion.46), channel_id=1, replica_groups=mesh['req'=32,'tp'=8] {'tp'}, use_global_device_ids=true, to_apply=%region_1.0 | all-reduce | flops 592 | bytes 4736 | tf_op jit(solution)/shard_map/psum | solution.py:83
  17.2 1.1 fusion.45
  18.4 1.2 dynamic_slice.7
  20.2 1.0 fusion.47
  21.5 0.9 dynamic_slice.8
  23.1 0.9 subtract_convert_fusion.1
  24.0 1.0 multiply_reduce_fusion.1
  25.4 84.1 %all_to_all.20 = bf16[32,136,384]{2,1,0:T(8,128)(2,1)S(1)} all-to-all(bf16[32,136,384]{2,1,0:T(8,128)(2,1)S(1)} %pad_maximum_fusion), channel_id=1, replica_groups=mesh['req'=32,'tp'=8] {'req'}, dimensions={0} | all-to-all | bytes 6684672 | tf_op jit(solution)/shard_map/all_to_all | solution.py:110
  109.5 6.0 %all-to-all-start.1 = ((bf16[32,128,384]{2,1,0:T(8,128)(2,1)}), bf16[32,128,384]{2,1,0:T(8,128)(2,1)}, u32[]{:S(2)}, u32[]{:S(2)}) async-start(bf16[32,128,384]{2,1,0:T(8,128)(2,1)} %bitcast.86), calls=%async_computation.1 | async-start | bytes 6291456 | tf_op jit(solution)/shard_map/all_to_all | solution.py:111
  115.6 2.3 copy.71
  118.5 2.3 copy.72
  120.9 1.5 fusion.56
  122.4 1.5 fusion.55
  124.5 0.7 iota_compare_fusion.2
  125.2 0.7 fusion.106
  125.9 0.7 bitcast_convert_fusion
  126.6 1.6 fusion.120
  128.1 1.6 fusion.122
  129.7 1.6 fusion.124
  131.3 0.8 reshape.270
  132.1 1.6 gather_fusion.1
  133.7 1.4 fusion.91
  135.2 0.8 fusion.103
  135.9 0.8 select_reduce_fusion
  136.7 0.8 fusion.104
  137.5 0.9 fusion.84
  138.5 1.6 fusion.89
  140.1 1.2 convolution_bitcast_fusion
  141.3 0.8 pad_maximum_fusion.1
  142.1 2.3 copy.73
  144.5 3.1 %reshape.301 = f32[32,1,3120]{2,1,0:T(1,128)} reshape(f32[256,3,130]{2,1,0:T(4,128)} %copy.73) | data formatting | bytes 798720
  148.5 3.0 %fusion.119 = (f32[288]{0:T(512)S(1)}, f32[288,4096]{1,0:T(8,128)}) fusion(bf16[4096,384]{1,0:T(8,128)(2,1)S(1)} %bitcast.80, bf16[288,384]{1,0:T(8,128)(2,1)S(1)} %bitcast.92, pred[4096]{0:T(1024)(128)(4,1)S(1)} %iota_compare_fusion.1), kind=kOutput, calls=%fused_computation.183 | convolution fusion | flops 305528544 | bytes 5846144 | tf_op jit(solution)/shard_map/qd,kd->qk/dot_general | solution.py:167
  151.6 3.1 %fusion.121 = (f32[288]{0:T(512)S(1)}, f32[288,4096]{1,0:T(8,128)}) fusion(bf16[4096,384]{1,0:T(8,128)(2,1)S(1)} %bitcast.81, bf16[288,384]{1,0:T(8,128)(2,1)S(1)} %bitcast.93, pred[4096]{0:T(1024)(128)(4,1)S(1)} %iota_compare_fusion.1), kind=kOutput, calls=%fused_computation.185 | convolution fusion | flops 305528544 | bytes 5846144 | tf_op jit(solution)/shard_map/qd,kd->qk/dot_general | solution.py:167
  154.6 3.0 %fusion.123 = (f32[288]{0:T(512)S(1)}, f32[288,4096]{1,0:T(8,128)}) fusion(bf16[4096,384]{1,0:T(8,128)(2,1)S(1)} %bitcast.82, bf16[288,384]{1,0:T(8,128)(2,1)S(1)} %bitcast.94, pred[4096]{0:T(1024)(128)(4,1)S(1)} %iota_compare_fusion.1), kind=kOutput, calls=%fused_computation.187 | convolution fusion | flops 305528544 | bytes 5846144 | tf_op jit(solution)/shard_map/qd,kd->qk/dot_general | solution.py:167
  157.7 23.4 %all-to-all-done.1 = bf16[32,128,384]{2,1,0:T(8,128)(2,1)} async-done(((bf16[32,128,384]{2,1,0:T(8,128)(2,1)}), bf16[32,128,384]{2,1,0:T(8,128)(2,1)}, u32[]{:S(2)}, u32[]{:S(2)}) %all-to-all-start.1) | async-done | bytes 3145760 | tf_op jit(solution)/shard_map/all_to_all | solution.py:111
  181.1 9.9 %all-to-all-start.2 = ((f32[32,1,3120]{2,1,0:T(1,128)}), f32[32,1,3120]{2,1,0:T(1,128)S(1)}, u32[]{:S(2)}, u32[]{:S(2)}) async-start(f32[32,1,3120]{2,1,0:T(1,128)} %reshape.301), calls=%async_computation.2 | async-start | bytes 819200 | tf_op jit(solution)/shard_map/all_to_all | solution.py:146
  191.0 3.6 %fusion.12 = f32[288,128]{1,0:T(8,128)S(1)} fusion(f32[288,4096]{1,0:T(8,128)} %get-tuple-element.30, f32[288]{0:T(512)S(1)} %max.26, pred[4096]{0:T(1024)(128)(4,1)S(1)} %iota_compare_fusion.1, bf16[4096,384]{1,0:T(8,128)(2,1)} %bitcast.4), kind=kOutput, calls=%fused_computation.23 | convolution fusion | flops 305528832 | bytes 5919872 | tf_op jit(solution)/shard_map/dot_general | solution.py:184
  194.7 4.3 %fusion.14 = f32[288,128]{1,0:T(8,128)S(1)} fusion(f32[288,4096]{1,0:T(8,128)} %get-tuple-element.38, f32[288]{0:T(512)S(1)} %max.25, pred[4096]{0:T(1024)(128)(4,1)S(1)} %iota_compare_fusion.1, bf16[4096,384]{1,0:T(8,128)(2,1)} %bitcast.4), kind=kOutput, calls=%fused_computation.24 | convolution fusion | flops 305528832 | bytes 5919872 | tf_op jit(solution)/shard_map/dot_general | solution.py:184
  199.8 2.6 fusion.6
  203.1 2.0 fusion.16
  206.0 1.6 reduce.3
  207.6 1.3 reshape.302
  210.7 3.9 %convert_bitcast_fusion = bf16[8,296,640]{2,1,0:T(8,128)(2,1)S(1)} fusion(bf16[48,8,8,640]{3,2,1,0:T(8,128)(2,1)} %bitcast.107, bf16[8,384]{1,0:T(8,128)(2,1)S(1)} %fusion.105, bf16[288,128]{1,0:T(8,128)(2,1)S(1)} %fusion.37, bf16[288,128]{1,0:T(8,128)(2,1)S(1)} %fusion.36, bf16[288,128]{1,0:T(8,128)(2,1)S(1)} %fusion.35), kind=kOutput, calls=%fused_computation.22 | convolution fusion | flops 1166344192 | bytes 7190528 | tf_op jit(solution)/shard_map/rk,kcn->crn/dot_general | solution.py:196
  214.6 48.9 %all_to_all.21 = bf16[8,296,640]{2,1,0:T(8,128)(2,1)S(1)} all-to-all(bf16[8,296,640]{2,1,0:T(8,128)(2,1)S(1)} %convert_bitcast_fusion), channel_id=1, replica_groups=mesh['req'=32,'tp'=8] {'tp'}, dimensions={0} | all-to-all | bytes 6062080 | tf_op jit(solution)/shard_map/all_to_all | solution.py:199
  264.1 12.7 %psum.23 = f32[296]{0:T(512)S(1)} all-reduce(f32[296]{0:T(512)S(1)} %multiply_reduce_fusion), channel_id=1, replica_groups=mesh['req'=32,'tp'=8] {'tp'}, use_global_device_ids=true, to_apply=%region_25.26 | all-reduce | flops 296 | bytes 2368 | tf_op jit(solution)/shard_map/psum | solution.py:203
  276.8 0.9 add_convert_fusion
  (110 shorter events, 8.9 us)
Async XLA Ops:
  21.4 3.6 %copy-start.1 = (bf16[32,1,128,384]{3,2,1,0:T(8,128)(2,1)S(1)}, bf16[32,1,128,384]{3,2,1,0:T(8,128)(2,1)}, u32[]{:S(2)}) copy-start(bf16[32,1,128,384]{3,2,1,0:T(8,128)(2,1)} %param.24) | copy-start | bytes 9437188
  23.9 1.0 copy-start.2
  23.9 1.0 copy-start.3
  24.0 1.0 copy-start.4
  24.0 1.0 copy-start.5
  109.5 8.3 %copy-start.18 = (s32[8]{0:T(128)S(1)}, s32[8]{0:T(128)}, u32[]{:S(2)}) copy-start(s32[8]{0:T(128)} %param.28) | copy-start | bytes 100
  109.5 8.4 %copy-start = (s32[256]{0:T(256)S(1)}, s32[256]{0:T(256)}, u32[]{:S(2)}) copy-start(s32[256]{0:T(256)} %param.30) | copy-start | bytes 3076
  109.5 71.6 %all-to-all-start.1 = ((bf16[32,128,384]{2,1,0:T(8,128)(2,1)}), bf16[32,128,384]{2,1,0:T(8,128)(2,1)}, u32[]{:S(2)}, u32[]{:S(2)}) async-start(bf16[32,128,384]{2,1,0:T(8,128)(2,1)} %bitcast.86), calls=%async_computation.1 | async-start | bytes 6291456 | tf_op jit(solution)/shard_map/all_to_all | solution.py:111
  115.6 9.0 %copy-start.20 = (s32[8]{0:T(128)S(1)}, s32[8]{0:T(128)}, u32[]{:S(2)}) copy-start(s32[8]{0:T(128)} %param.29) | copy-start | bytes 100
  117.9 11.8 %copy-start.13 = (s32[1024]{0:T(1024)}, s32[1024]{0:T(1024)S(1)}, u32[]{:S(2)}) copy-start(s32[1024]{0:T(1024)S(1)} %pad_clamp_fusion) | copy-start | bytes 12292
  122.4 7.4 %copy-start.6 = (bf16[36,8,3,128]{3,1,2,0:T(8,128)(2,1)}, bf16[36,8,3,128]{3,1,2,0:T(8,128)(2,1)S(1)}, u32[]{:S(2)}) copy-start(bf16[36,8,3,128]{3,1,2,0:T(8,128)(2,1)S(1)} %copy.127) | copy-start | bytes 663556
  147.5 0.9 copy-start.7
  148.5 3.0 %copy-start.17 = (f32[288]{0:T(512)S(1)}, f32[288]{0:T(512)}, u32[]{:S(2)}) copy-start(f32[288]{0:T(512)} %get-tuple-element.31) | copy-start | bytes 3460
  148.5 3.0 %copy-start.10 = (f32[288,288]{0,1:T(8,128)S(1)}, f32[288,288]{0,1:T(8,128)}, u32[]{:S(2)}) copy-start(f32[288,288]{0,1:T(8,128)} %get-tuple-element.32) | copy-start | bytes 995332
  181.1 13.6 %copy-start.16 = (f32[288]{0:T(512)S(1)}, f32[288]{0:T(512)}, u32[]{:S(2)}) copy-start(f32[288]{0:T(512)} %get-tuple-element.39) | copy-start | bytes 3460
  181.1 24.4 %all-to-all-start.2 = ((f32[32,1,3120]{2,1,0:T(1,128)}), f32[32,1,3120]{2,1,0:T(1,128)S(1)}, u32[]{:S(2)}, u32[]{:S(2)}) async-start(f32[32,1,3120]{2,1,0:T(1,128)} %reshape.301), calls=%async_computation.2 | async-start | bytes 819200 | tf_op jit(solution)/shard_map/all_to_all | solution.py:146
  191.0 8.1 %slice-start = ((s8[4718592]{0:T(1024)(128)(4,1)}), s8[4194304]{0:T(1024)(128)(4,1)S(1)}, s32[]{:S(2)}) async-start(s8[4718592]{0:T(1024)(128)(4,1)} %bitcast.74), calls=%async_computation.4 | async-start | bytes 8388608
  191.0 8.1 %slice-start.2 = ((s8[4718592]{0:T(1024)(128)(4,1)}), s8[4194304]{0:T(1024)(128)(4,1)S(1)}, s32[]{:S(2)}) async-start(s8[4718592]{0:T(1024)(128)(4,1)} %bitcast.76), calls=%async_computation.6 | async-start | bytes 8388608
  191.0 8.2 %slice-start.4 = ((s8[4718592]{0:T(1024)(128)(4,1)}), s8[4194304]{0:T(1024)(128)(4,1)S(1)}, s32[]{:S(2)}) async-start(s8[4718592]{0:T(1024)(128)(4,1)} %bitcast.78), calls=%async_computation.8 | async-start | bytes 8388608
  194.7 4.3 %copy-start.9 = (f32[288,288]{0,1:T(8,128)S(1)}, f32[288,288]{0,1:T(8,128)}, u32[]{:S(2)}) copy-start(f32[288,288]{0,1:T(8,128)} %get-tuple-element.40) | copy-start | bytes 995332
  194.7 4.4 %copy-start.15 = (f32[288]{0:T(512)S(1)}, f32[288]{0:T(512)}, u32[]{:S(2)}) copy-start(f32[288]{0:T(512)} %get-tuple-element.35) | copy-start | bytes 3460
  194.7 4.8 %slice-start.1 = ((s8[4718592]{0:T(1024)(128)(4,1)}), s8[524288]{0:T(1024)(128)(4,1)S(1)}, s32[]{:S(2)}) async-start(s8[4718592]{0:T(1024)(128)(4,1)} %bitcast.74), calls=%async_computation.5 | async-start | bytes 1048576
  194.7 4.9 %slice-start.3 = ((s8[4718592]{0:T(1024)(128)(4,1)}), s8[524288]{0:T(1024)(128)(4,1)S(1)}, s32[]{:S(2)}) async-start(s8[4718592]{0:T(1024)(128)(4,1)} %bitcast.76), calls=%async_computation.7 | async-start | bytes 1048576
  194.7 5.1 %slice-start.5 = ((s8[4718592]{0:T(1024)(128)(4,1)}), s8[524288]{0:T(1024)(128)(4,1)S(1)}, s32[]{:S(2)}) async-start(s8[4718592]{0:T(1024)(128)(4,1)} %bitcast.78), calls=%async_computation.9 | async-start | bytes 1048576
  199.8 2.7 copy-start.19
  199.8 3.2 %copy-start.8 = (f32[288,288]{0,1:T(8,128)S(1)}, f32[288,288]{0,1:T(8,128)}, u32[]{:S(2)}) copy-start(f32[288,288]{0,1:T(8,128)} %get-tuple-element.36) | copy-start | bytes 995332
  205.2 4.5 %copy-start.12 = (f32[8,3]{1,0:T(8,128)S(1)}, f32[8,3]{1,0:T(8,128)}, u32[]{:S(2)}) copy-start(f32[8,3]{1,0:T(8,128)} %get-tuple-element.12) | copy-start | bytes 292
  214.6 62.2 %copy-start.11 = (bf16[296,640]{1,0:T(8,128)(2,1)S(1)}, bf16[296,640]{1,0:T(8,128)(2,1)}, u32[]{:S(2)}) copy-start(bf16[296,640]{1,0:T(8,128)(2,1)} %param.16) | copy-start | bytes 1136644
  214.6 62.2 %copy-start.14 = (f32[640]{0:T(1024)S(1)}, f32[640]{0:T(1024)}, u32[]{:S(2)}) copy-start(f32[640]{0:T(1024)} %param.23) | copy-start | bytes 7684

commit v3 on v2

--- a/solution.py
+++ b/solution.py
@@ -200,7 +200,11 @@
         partial.astype(jnp.bfloat16), "tp", split_axis=0, concat_axis=0, tiled=True
     )
     my_share = jnp.sum(pieces.astype(jnp.float32), 0)
-    power = lax.psum(jnp.sum(my_share * my_share, 1), "tp")
+    power_part = jnp.sum(my_share * my_share, 1)
+    power_copies = jnp.broadcast_to(power_part[None], (tp_count, power_part.shape[0]))
+    power = jnp.sum(
+        lax.all_to_all(power_copies, "tp", split_axis=0, concat_axis=0, tiled=True), 0
+    )
     inverse = lax.rsqrt(power / (share_width * tp_count) + EPSILON)
     normed = my_share * inverse[:, None]
     return (hidden.astype(jnp.float32) + normed * post_gain[None, :]).astype(jnp.bfloat16)

time: 279 us -> 274 us (0.982)
  blocking collectives: 161 us -> 156 us
    psum x1 -> x0, blocking collectives: 12.7 us -> none  [body(): power = lax.psum(jnp.sum(my_share * my_share, 1), 'tp')]
    all_to_all x0 -> x1, blocking collectives: none -> 7.88 us  [body(): lax.all_to_all(power_copies, 'tp', split_axis=0, concat_axis=0, tiled=True)]
where the time goes in v3:
time: 274 us; the launch traced here: 273 us
  blocking collectives  156 us (57%)
  matrix products  33.6 us (12%)
  waiting for transfers between devices  23.4 us (9%)
  other arithmetic  23.2 us (8%)
  local copies, waits for them, and re-layouts  20.2 us (7%)
  starting transfers between devices  16 us (6%)
    all_to_all x1, blocking collectives, body(): lax.all_to_all(outgoing, 'req', split_axis=0, concat_axis=0, tiled=True)  84.1 us
    all_to_all x1, blocking collectives, body(): lax.all_to_all(partial.astype(jnp.bfloat16), 'tp', split_axis=0, concat_a...  48.9 us
    all_to_all x1, waiting for transfers between devices, body(): lax.all_to_all(prefix_values.reshape(groups, block_rows, local_width), 'r...  23.4 us
    psum x1, blocking collectives, body(): lax.psum((jnp.sum(float_query * float_query, 1), jnp.sum(float_key * floa...  15 us
    unnamed x61, local copies, waits for them, and re-layouts  10.2 us
    dot_general x3, matrix products, body(): jnp.dot(pre_exp.astype(jnp.bfloat16), own_values[:, cols], preferred_elem...  9.94 us
    all_to_all x1, starting transfers between devices, body(): lax.all_to_all(packed, 'req', split_axis=0, concat_axis=0, tiled=True)  9.92 us
    dot_general x3, matrix products, body(): jnp.einsum('qd,kd->qk', head_query, own_keys[:, cols], preferred_element_...  9.08 us
  transfers between devices with their start and end apart: 2, of which 1 were waited for; matrix products, arithmetic and copies ran while one was open for 20% of the time, Pallas kernels for 0%

profile of v3, /device:TPU:1, one launch (start us, length us, event | category | flops | bytes accessed | tf_op | source)
XLA Modules:
  0.0 273.0 jit_solution(18097125276707340496)
XLA Ops:
  0.0 1.1 fusion.44
  1.1 1.1 fusion.46
  2.2 15.0 %all-reduce.1 = (f32[296]{0:T(512)S(1)}, f32[296]{0:T(512)S(1)}) all-reduce(f32[296]{0:T(512)S(1)} %fusion.44, f32[296]{0:T(512)S(1)} %fusion.46), channel_id=1, replica_groups=mesh['req'=32,'tp'=8] {'tp'}, use_global_device_ids=true, to_apply=%region_1.0 | all-reduce | flops 592 | bytes 4736 | tf_op jit(solution)/shard_map/psum | solution.py:83
  17.2 1.1 fusion.45
  18.4 1.2 dynamic_slice.7
  20.2 1.0 fusion.47
  21.5 0.9 dynamic_slice.8
  23.1 0.9 subtract_convert_fusion.1
  24.0 1.0 multiply_reduce_fusion.1
  25.4 84.1 %all_to_all.26 = bf16[32,136,384]{2,1,0:T(8,128)(2,1)S(1)} all-to-all(bf16[32,136,384]{2,1,0:T(8,128)(2,1)S(1)} %pad_maximum_fusion), channel_id=1, replica_groups=mesh['req'=32,'tp'=8] {'req'}, dimensions={0} | all-to-all | bytes 6684672 | tf_op jit(solution)/shard_map/all_to_all | solution.py:110
  109.5 6.0 %all-to-all-start.1 = ((bf16[32,128,384]{2,1,0:T(8,128)(2,1)}), bf16[32,128,384]{2,1,0:T(8,128)(2,1)}, u32[]{:S(2)}, u32[]{:S(2)}) async-start(bf16[32,128,384]{2,1,0:T(8,128)(2,1)} %bitcast.86), calls=%async_computation.1 | async-start | bytes 6291456 | tf_op jit(solution)/shard_map/all_to_all | solution.py:111
  115.6 2.3 copy.83
  118.5 2.3 copy.84
  120.9 1.5 fusion.56
  122.4 1.5 fusion.55
  124.5 0.7 iota_compare_fusion.2
  125.2 0.7 fusion.106
  125.9 0.7 bitcast_convert_fusion
  126.6 1.6 fusion.120
  128.1 1.6 fusion.122
  129.7 1.6 fusion.124
  131.3 0.8 reshape.280
  132.1 1.6 gather_fusion.1
  133.7 1.4 fusion.91
  135.2 0.8 fusion.103
  135.9 0.8 select_reduce_fusion
  136.7 0.8 fusion.104
  137.5 0.9 fusion.84
  138.5 1.6 fusion.89
  140.1 1.2 convolution_bitcast_fusion
  141.3 0.8 pad_maximum_fusion.1
  142.1 2.3 copy.85
  144.5 3.1 %reshape.311 = f32[32,1,3120]{2,1,0:T(1,128)} reshape(f32[256,3,130]{2,1,0:T(4,128)} %copy.85) | data formatting | bytes 798720
  148.5 3.0 %fusion.119 = (f32[288]{0:T(512)S(1)}, f32[288,4096]{1,0:T(8,128)}) fusion(bf16[4096,384]{1,0:T(8,128)(2,1)S(1)} %bitcast.80, bf16[288,384]{1,0:T(8,128)(2,1)S(1)} %bitcast.92, pred[4096]{0:T(1024)(128)(4,1)S(1)} %iota_compare_fusion.1), kind=kOutput, calls=%fused_computation.183 | convolution fusion | flops 305528544 | bytes 5846144 | tf_op jit(solution)/shard_map/qd,kd->qk/dot_general | solution.py:167
  151.6 3.1 %fusion.121 = (f32[288]{0:T(512)S(1)}, f32[288,4096]{1,0:T(8,128)}) fusion(bf16[4096,384]{1,0:T(8,128)(2,1)S(1)} %bitcast.81, bf16[288,384]{1,0:T(8,128)(2,1)S(1)} %bitcast.93, pred[4096]{0:T(1024)(128)(4,1)S(1)} %iota_compare_fusion.1), kind=kOutput, calls=%fused_computation.185 | convolution fusion | flops 305528544 | bytes 5846144 | tf_op jit(solution)/shard_map/qd,kd->qk/dot_general | solution.py:167
  154.6 3.0 %fusion.123 = (f32[288]{0:T(512)S(1)}, f32[288,4096]{1,0:T(8,128)}) fusion(bf16[4096,384]{1,0:T(8,128)(2,1)S(1)} %bitcast.82, bf16[288,384]{1,0:T(8,128)(2,1)S(1)} %bitcast.94, pred[4096]{0:T(1024)(128)(4,1)S(1)} %iota_compare_fusion.1), kind=kOutput, calls=%fused_computation.187 | convolution fusion | flops 305528544 | bytes 5846144 | tf_op jit(solution)/shard_map/qd,kd->qk/dot_general | solution.py:167
  157.7 23.4 %all-to-all-done.1 = bf16[32,128,384]{2,1,0:T(8,128)(2,1)} async-done(((bf16[32,128,384]{2,1,0:T(8,128)(2,1)}), bf16[32,128,384]{2,1,0:T(8,128)(2,1)}, u32[]{:S(2)}, u32[]{:S(2)}) %all-to-all-start.1) | async-done | bytes 3145760 | tf_op jit(solution)/shard_map/all_to_all | solution.py:111
  181.1 9.9 %all-to-all-start.2 = ((f32[32,1,3120]{2,1,0:T(1,128)}), f32[32,1,3120]{2,1,0:T(1,128)S(1)}, u32[]{:S(2)}, u32[]{:S(2)}) async-start(f32[32,1,3120]{2,1,0:T(1,128)} %reshape.311), calls=%async_computation.2 | async-start | bytes 819200 | tf_op jit(solution)/shard_map/all_to_all | solution.py:146
  191.0 3.6 %fusion.12 = f32[288,128]{1,0:T(8,128)S(1)} fusion(f32[288,4096]{1,0:T(8,128)} %get-tuple-element.30, f32[288]{0:T(512)S(1)} %max.26, pred[4096]{0:T(1024)(128)(4,1)S(1)} %iota_compare_fusion.1, bf16[4096,384]{1,0:T(8,128)(2,1)} %bitcast.4), kind=kOutput, calls=%fused_computation.23 | convolution fusion | flops 305528832 | bytes 5919872 | tf_op jit(solution)/shard_map/dot_general | solution.py:184
  194.7 4.3 %fusion.14 = f32[288,128]{1,0:T(8,128)S(1)} fusion(f32[288,4096]{1,0:T(8,128)} %get-tuple-element.38, f32[288]{0:T(512)S(1)} %max.25, pred[4096]{0:T(1024)(128)(4,1)S(1)} %iota_compare_fusion.1, bf16[4096,384]{1,0:T(8,128)(2,1)} %bitcast.4), kind=kOutput, calls=%fused_computation.24 | convolution fusion | flops 305528832 | bytes 5919872 | tf_op jit(solution)/shard_map/dot_general | solution.py:184
  199.8 2.6 fusion.6
  203.1 2.0 fusion.16
  206.0 1.6 reduce.4
  207.6 1.3 reshape.312
  210.7 3.9 %convert_bitcast_fusion = bf16[8,296,640]{2,1,0:T(8,128)(2,1)S(1)} fusion(bf16[48,8,8,640]{3,2,1,0:T(8,128)(2,1)} %bitcast.107, bf16[8,384]{1,0:T(8,128)(2,1)S(1)} %fusion.105, bf16[288,128]{1,0:T(8,128)(2,1)S(1)} %fusion.37, bf16[288,128]{1,0:T(8,128)(2,1)S(1)} %fusion.36, bf16[288,128]{1,0:T(8,128)(2,1)S(1)} %fusion.35), kind=kOutput, calls=%fused_computation.22 | convolution fusion | flops 1166344192 | bytes 7190528 | tf_op jit(solution)/shard_map/rk,kcn->crn/dot_general | solution.py:196
  214.6 48.9 %all_to_all.27 = bf16[8,296,640]{2,1,0:T(8,128)(2,1)S(1)} all-to-all(bf16[8,296,640]{2,1,0:T(8,128)(2,1)S(1)} %convert_bitcast_fusion), channel_id=1, replica_groups=mesh['req'=32,'tp'=8] {'tp'}, dimensions={0} | all-to-all | bytes 6062080 | tf_op jit(solution)/shard_map/all_to_all | solution.py:199
  264.1 7.9 %all_to_all.28 = f32[8,1,296]{2,1,0:T(1,128)S(1)} all-to-all(f32[8,1,296]{2,1,0:T(1,128)S(1)} %broadcast_in_dim.179), channel_id=1, replica_groups=mesh['req'=32,'tp'=8] {'tp'}, dimensions={0} | all-to-all | bytes 18944 | tf_op jit(solution)/shard_map/all_to_all | solution.py:206
  272.0 0.9 add_convert_fusion
  (112 shorter events, 8.9 us)
Async XLA Ops:
  21.4 3.6 %copy-start.1 = (bf16[32,1,128,384]{3,2,1,0:T(8,128)(2,1)S(1)}, bf16[32,1,128,384]{3,2,1,0:T(8,128)(2,1)}, u32[]{:S(2)}) copy-start(bf16[32,1,128,384]{3,2,1,0:T(8,128)(2,1)} %param.24) | copy-start | bytes 9437188
  23.9 1.0 copy-start.2
  23.9 1.0 copy-start.3
  24.0 1.0 copy-start.4
  24.0 1.0 copy-start.5
  109.5 8.3 %copy-start.18 = (s32[8]{0:T(128)S(1)}, s32[8]{0:T(128)}, u32[]{:S(2)}) copy-start(s32[8]{0:T(128)} %param.28) | copy-start | bytes 100
  109.5 8.4 %copy-start = (s32[256]{0:T(256)S(1)}, s32[256]{0:T(256)}, u32[]{:S(2)}) copy-start(s32[256]{0:T(256)} %param.30) | copy-start | bytes 3076
  109.5 71.6 %all-to-all-start.1 = ((bf16[32,128,384]{2,1,0:T(8,128)(2,1)}), bf16[32,128,384]{2,1,0:T(8,128)(2,1)}, u32[]{:S(2)}, u32[]{:S(2)}) async-start(bf16[32,128,384]{2,1,0:T(8,128)(2,1)} %bitcast.86), calls=%async_computation.1 | async-start | bytes 6291456 | tf_op jit(solution)/shard_map/all_to_all | solution.py:111
  115.6 9.0 %copy-start.20 = (s32[8]{0:T(128)S(1)}, s32[8]{0:T(128)}, u32[]{:S(2)}) copy-start(s32[8]{0:T(128)} %param.29) | copy-start | bytes 100
  117.9 11.8 %copy-start.13 = (s32[1024]{0:T(1024)}, s32[1024]{0:T(1024)S(1)}, u32[]{:S(2)}) copy-start(s32[1024]{0:T(1024)S(1)} %pad_clamp_fusion) | copy-start | bytes 12292
  122.4 7.4 %copy-start.6 = (bf16[36,8,3,128]{3,1,2,0:T(8,128)(2,1)}, bf16[36,8,3,128]{3,1,2,0:T(8,128)(2,1)S(1)}, u32[]{:S(2)}) copy-start(bf16[36,8,3,128]{3,1,2,0:T(8,128)(2,1)S(1)} %copy.141) | copy-start | bytes 663556
  147.5 0.9 copy-start.7
  148.5 3.0 %copy-start.17 = (f32[288]{0:T(512)S(1)}, f32[288]{0:T(512)}, u32[]{:S(2)}) copy-start(f32[288]{0:T(512)} %get-tuple-element.31) | copy-start | bytes 3460
  148.5 3.0 %copy-start.10 = (f32[288,288]{0,1:T(8,128)S(1)}, f32[288,288]{0,1:T(8,128)}, u32[]{:S(2)}) copy-start(f32[288,288]{0,1:T(8,128)} %get-tuple-element.32) | copy-start | bytes 995332
  181.1 13.6 %copy-start.16 = (f32[288]{0:T(512)S(1)}, f32[288]{0:T(512)}, u32[]{:S(2)}) copy-start(f32[288]{0:T(512)} %get-tuple-element.39) | copy-start | bytes 3460
  181.1 24.4 %all-to-all-start.2 = ((f32[32,1,3120]{2,1,0:T(1,128)}), f32[32,1,3120]{2,1,0:T(1,128)S(1)}, u32[]{:S(2)}, u32[]{:S(2)}) async-start(f32[32,1,3120]{2,1,0:T(1,128)} %reshape.311), calls=%async_computation.2 | async-start | bytes 819200 | tf_op jit(solution)/shard_map/all_to_all | solution.py:146
  191.0 8.1 %slice-start = ((s8[4718592]{0:T(1024)(128)(4,1)}), s8[4194304]{0:T(1024)(128)(4,1)S(1)}, s32[]{:S(2)}) async-start(s8[4718592]{0:T(1024)(128)(4,1)} %bitcast.74), calls=%async_computation.5 | async-start | bytes 8388608
  191.0 8.1 %slice-start.2 = ((s8[4718592]{0:T(1024)(128)(4,1)}), s8[4194304]{0:T(1024)(128)(4,1)S(1)}, s32[]{:S(2)}) async-start(s8[4718592]{0:T(1024)(128)(4,1)} %bitcast.76), calls=%async_computation.7 | async-start | bytes 8388608
  191.0 8.2 %slice-start.4 = ((s8[4718592]{0:T(1024)(128)(4,1)}), s8[4194304]{0:T(1024)(128)(4,1)S(1)}, s32[]{:S(2)}) async-start(s8[4718592]{0:T(1024)(128)(4,1)} %bitcast.78), calls=%async_computation.9 | async-start | bytes 8388608
  194.7 4.3 %copy-start.9 = (f32[288,288]{0,1:T(8,128)S(1)}, f32[288,288]{0,1:T(8,128)}, u32[]{:S(2)}) copy-start(f32[288,288]{0,1:T(8,128)} %get-tuple-element.40) | copy-start | bytes 995332
  194.7 4.4 %copy-start.15 = (f32[288]{0:T(512)S(1)}, f32[288]{0:T(512)}, u32[]{:S(2)}) copy-start(f32[288]{0:T(512)} %get-tuple-element.35) | copy-start | bytes 3460
  194.7 4.8 %slice-start.1 = ((s8[4718592]{0:T(1024)(128)(4,1)}), s8[524288]{0:T(1024)(128)(4,1)S(1)}, s32[]{:S(2)}) async-start(s8[4718592]{0:T(1024)(128)(4,1)} %bitcast.74), calls=%async_computation.6 | async-start | bytes 1048576
  194.7 4.9 %slice-start.3 = ((s8[4718592]{0:T(1024)(128)(4,1)}), s8[524288]{0:T(1024)(128)(4,1)S(1)}, s32[]{:S(2)}) async-start(s8[4718592]{0:T(1024)(128)(4,1)} %bitcast.76), calls=%async_computation.8 | async-start | bytes 1048576
  194.7 5.1 %slice-start.5 = ((s8[4718592]{0:T(1024)(128)(4,1)}), s8[524288]{0:T(1024)(128)(4,1)S(1)}, s32[]{:S(2)}) async-start(s8[4718592]{0:T(1024)(128)(4,1)} %bitcast.78), calls=%async_computation.10 | async-start | bytes 1048576
  199.8 2.7 copy-start.19
  199.8 3.2 %copy-start.8 = (f32[288,288]{0,1:T(8,128)S(1)}, f32[288,288]{0,1:T(8,128)}, u32[]{:S(2)}) copy-start(f32[288,288]{0,1:T(8,128)} %get-tuple-element.36) | copy-start | bytes 995332
  205.2 4.5 %copy-start.12 = (f32[8,3]{1,0:T(8,128)S(1)}, f32[8,3]{1,0:T(8,128)}, u32[]{:S(2)}) copy-start(f32[8,3]{1,0:T(8,128)} %get-tuple-element.12) | copy-start | bytes 292
  214.6 57.4 %copy-start.11 = (bf16[296,640]{1,0:T(8,128)(2,1)S(1)}, bf16[296,640]{1,0:T(8,128)(2,1)}, u32[]{:S(2)}) copy-start(bf16[296,640]{1,0:T(8,128)(2,1)} %param.16) | copy-start | bytes 1136644
  214.6 57.4 %copy-start.14 = (f32[640]{0:T(1024)S(1)}, f32[640]{0:T(1024)}, u32[]{:S(2)}) copy-start(f32[640]{0:T(1024)} %param.23) | copy-start | bytes 7684
